TPU v7x, 32 devices: a whole 2x2x4 slice. The times are simulated.
32 devices in a mesh: dp: 16 (over z, y, core), pair: 2 (over x).
Axes of the slice: x: 2, y: 2, z: 4, core: 2. Of those that a mesh axis runs over, the one named last changes fastest.
Arguments:
- latents: bfloat16 [64, 256, 768], P(('dp', 'pair')), may hold values from -6 to 6
- conditioning: bfloat16 [64, 768], P(('dp', 'pair')), may hold values from -6 to 6
- cotangent: bfloat16 [64, 256, 768], P(('dp', 'pair')), may hold values from -6 to 6
- adaln_weight: bfloat16 [2, 768, 4608], P(None, ('dp', 'pair')), may hold values from -0.21875 to 0.21875
- adaln_bias: bfloat16 [2, 4608], P(None, ('dp', 'pair')), may hold values from -3 to 3
- qkv_weight: bfloat16 [2, 768, 2304], P(None, ('dp', 'pair')), may hold values from -0.21875 to 0.21875
- query_bias: bfloat16 [2, 768], P(None, ('dp', 'pair')), may hold values from -3 to 3
- value_bias: bfloat16 [2, 768], P(None, ('dp', 'pair')), may hold values from -3 to 3
- proj_weight: bfloat16 [2, 768, 768], P(None, ('dp', 'pair')), may hold values from -0.875 to 0.875
- proj_bias: bfloat16 [2, 768], P(None, ('dp', 'pair')), may hold values from -3 to 3
- expand_weight: bfloat16 [2, 768, 3072], P(None, ('dp', 'pair')), may hold values from -0.21875 to 0.21875
- expand_bias: bfloat16 [2, 3072], P(None, ('dp', 'pair')), may hold values from -3 to 3
- reduce_weight: bfloat16 [2, 3072, 768], P(None, ('dp', 'pair')), may hold values from -0.109375 to 0.109375
- reduce_bias: bfloat16 [2, 768], P(None, ('dp', 'pair')), may hold values from -3 to 3
Outputs:
- outputs: bfloat16 [64, 256, 768], P(('dp', 'pair'))
- grad_latents: float32 [64, 256, 768], P(('dp', 'pair'))
- grad_conditioning: float32 [64, 768], P(('dp', 'pair'))
- grad_adaln_weight: float32 [2, 768, 4608], P(None, ('dp', 'pair'))
- grad_adaln_bias: float32 [2, 4608], P(None, ('dp', 'pair'))
- grad_qkv_weight: float32 [2, 768, 2304], P(None, ('dp', 'pair'))
- grad_query_bias: float32 [2, 768], P(None, ('dp', 'pair'))
- grad_value_bias: float32 [2, 768], P(None, ('dp', 'pair'))
- grad_proj_weight: float32 [2, 768, 768], P(None, ('dp', 'pair'))
- grad_proj_bias: float32 [2, 768], P(None, ('dp', 'pair'))
- grad_expand_weight: float32 [2, 768, 3072], P(None, ('dp', 'pair'))
- grad_expand_bias: float32 [2, 3072], P(None, ('dp', 'pair'))
- grad_reduce_weight: float32 [2, 3072, 768], P(None, ('dp', 'pair'))
- grad_reduce_bias: float32 [2, 768], P(None, ('dp', 'pair'))
All inputs are finite; a program needn't handle non-finite values.
Results may differ from a plain program's by a relative error of at most 0.025.
The roundings to bfloat16 on the way count: a program that leaves them out, or rounds other values in their place, can miss the bound.
Values may be sent and summed in bfloat16 or wider, within the bound.
A program may use at most 256 MiB of HBM per device.

v0:
```python
import jax
import jax.numpy as jnp
from jax import lax
from jax.sharding import PartitionSpec as P

HEADS = 12
HEAD = 64
LAYERS = 2
MB = 2


EPSILON = 1e-06


def layer_norm(values):
    centre = values - jnp.mean(values, axis=-1, keepdims=True)
    spread = jnp.mean(centre * centre, axis=-1, keepdims=True)
    return centre * lax.rsqrt(spread + EPSILON)


def modulate(residual_state, shift, scale):
    return layer_norm(residual_state) * (1.0 + scale[:, None, :]) + shift[:, None, :]


def gelu_tanh(values):
    return jax.nn.gelu(values, approximate=True)


def fetch_forward(shards, layer_number):
    (
        adaln_weight,
        adaln_bias,
        qkv_weight,
        query_bias,
        value_bias,
        proj_weight,
        proj_bias,
        expand_weight,
        expand_bias,
        reduce_weight,
        reduce_bias,
    ) = shards
    return (
        lax.all_gather(adaln_weight[layer_number], ("dp", "pair"), axis=0, tiled=True),
        lax.all_gather(adaln_bias[layer_number], ("dp", "pair"), axis=0, tiled=True),
        lax.all_gather(qkv_weight[layer_number], ("dp", "pair"), axis=0, tiled=True),
        lax.all_gather(query_bias[layer_number], ("dp", "pair"), axis=0, tiled=True),
        lax.all_gather(value_bias[layer_number], ("dp", "pair"), axis=0, tiled=True),
        lax.all_gather(proj_weight[layer_number], ("dp", "pair"), axis=0, tiled=True),
        lax.all_gather(proj_bias[layer_number], ("dp", "pair"), axis=0, tiled=True),
        lax.all_gather(expand_weight[layer_number], ("dp", "pair"), axis=0, tiled=True),
        lax.all_gather(expand_bias[layer_number], ("dp", "pair"), axis=0, tiled=True),
        lax.all_gather(reduce_weight[layer_number], ("dp", "pair"), axis=0, tiled=True),
        lax.all_gather(reduce_bias[layer_number], ("dp", "pair"), axis=0, tiled=True),
    )


def fetch_backward(shards, layer_number):
    (
        adaln_weight,
        adaln_bias,
        qkv_weight,
        query_bias,
        value_bias,
        proj_weight,
        proj_bias,
        expand_weight,
        expand_bias,
        reduce_weight,
        reduce_bias,
    ) = shards
    return (
        lax.all_gather(adaln_weight[layer_number], ("dp", "pair"), axis=0, tiled=True),
        lax.all_gather(adaln_bias[layer_number], ("dp", "pair"), axis=0, tiled=True),
        lax.all_gather(qkv_weight[layer_number], ("dp", "pair"), axis=0, tiled=True),
        lax.all_gather(query_bias[layer_number], ("dp", "pair"), axis=0, tiled=True),
        lax.all_gather(value_bias[layer_number], ("dp", "pair"), axis=0, tiled=True),
        lax.all_gather(proj_weight[layer_number], ("dp", "pair"), axis=0, tiled=True),
        lax.all_gather(proj_bias[layer_number], ("dp", "pair"), axis=0, tiled=True),
        lax.all_gather(expand_weight[layer_number], ("dp", "pair"), axis=0, tiled=True),
        lax.all_gather(expand_bias[layer_number], ("dp", "pair"), axis=0, tiled=True),
        lax.all_gather(reduce_weight[layer_number], ("dp", "pair"), axis=0, tiled=True),
        lax.all_gather(reduce_bias[layer_number], ("dp", "pair"), axis=0, tiled=True),
    )


def tile_rows(matrix):
    if matrix.ndim == 2:
        return matrix.reshape(matrix.shape[0] * matrix.shape[1] // 128, 128)
    return matrix


def untile_rows(matrix, columns):
    if columns > 0:
        return matrix.reshape(-1, columns)
    return matrix


def send_grads(totals):
    widths = [member.shape[1] if member.ndim == 2 else 0 for member in totals]
    flat = [tile_rows(member) for member in totals]
    summed = (
        lax.psum_scatter(flat[0], ("dp", "pair"), scatter_dimension=0, tiled=True),
        lax.psum_scatter(flat[1], ("dp", "pair"), scatter_dimension=0, tiled=True),
        lax.psum_scatter(flat[2], ("dp", "pair"), scatter_dimension=0, tiled=True),
        lax.psum_scatter(flat[3], ("dp", "pair"), scatter_dimension=0, tiled=True),
        lax.psum_scatter(flat[4], ("dp", "pair"), scatter_dimension=0, tiled=True),
        lax.psum_scatter(flat[5], ("dp", "pair"), scatter_dimension=0, tiled=True),
        lax.psum_scatter(flat[6], ("dp", "pair"), scatter_dimension=0, tiled=True),
        lax.psum_scatter(flat[7], ("dp", "pair"), scatter_dimension=0, tiled=True),
        lax.psum_scatter(flat[8], ("dp", "pair"), scatter_dimension=0, tiled=True),
        lax.psum_scatter(flat[9], ("dp", "pair"), scatter_dimension=0, tiled=True),
        lax.psum_scatter(flat[10], ("dp", "pair"), scatter_dimension=0, tiled=True),
    )
    return tuple((untile_rows(member, columns) for member, columns in zip(summed, widths)))


def forward_layer(residual_state, cond_part, gathered):
    (
        adaln_weight,
        adaln_bias,
        qkv_weight,
        query_bias,
        value_bias,
        proj_weight,
        proj_bias,
        expand_weight,
        expand_bias,
        reduce_weight,
        reduce_bias,
    ) = gathered
    latent_count, seq_len, model_width = residual_state.shape
    inv_root = HEAD ** (-0.5)
    silu_low = jax.nn.silu(cond_part).astype(jnp.bfloat16)
    modulation = jnp.dot(
        silu_low, adaln_weight, preferred_element_type=jnp.float32
    ) + adaln_bias.astype(jnp.float32)
    shift_attn, scale_attn, gate_attn, shift_mlp, scale_mlp, gate_mlp = jnp.split(
        modulation, 6, axis=-1
    )
    normed_in = modulate(residual_state, shift_attn, scale_attn).astype(jnp.bfloat16)
    qkv_bias = jnp.concatenate([query_bias, jnp.zeros_like(query_bias), value_bias]).astype(
        jnp.float32
    )
    qkv_rows = (
        jnp.dot(normed_in, qkv_weight, preferred_element_type=jnp.float32) + qkv_bias
    ).astype(jnp.bfloat16)
    qkv_rows = qkv_rows.reshape(latent_count, seq_len, 3, HEADS, HEAD)
    scores = (
        jnp.einsum(
            "bqhe,bkhe->bhqk",
            qkv_rows[:, :, 0],
            qkv_rows[:, :, 1],
            preferred_element_type=jnp.float32,
        )
        * inv_root
    )
    top_score = jnp.max(scores, axis=-1, keepdims=True)
    weights_exp = jnp.exp(scores - top_score)
    total_exp = jnp.sum(weights_exp, axis=-1, keepdims=True)
    probs = weights_exp / total_exp
    log_total = top_score + jnp.log(total_exp)
    attended = jnp.einsum(
        "bhqk,bkhe->bqhe",
        probs.astype(jnp.bfloat16),
        qkv_rows[:, :, 2],
        preferred_element_type=jnp.float32,
    )
    attended = attended.astype(jnp.bfloat16).reshape(latent_count, seq_len, model_width)
    attn_out = jnp.dot(
        attended, proj_weight, preferred_element_type=jnp.float32
    ) + proj_bias.astype(jnp.float32)
    middle = residual_state + gate_attn[:, None, :] * attn_out
    normed_mid = modulate(middle, shift_mlp, scale_mlp).astype(jnp.bfloat16)
    pre_act = jnp.dot(
        normed_mid, expand_weight, preferred_element_type=jnp.float32
    ) + expand_bias.astype(jnp.float32)
    activated = gelu_tanh(pre_act).astype(jnp.bfloat16)
    mlp_out = jnp.dot(
        activated, reduce_weight, preferred_element_type=jnp.float32
    ) + reduce_bias.astype(jnp.float32)
    result = middle + gate_mlp[:, None, :] * mlp_out
    stored = (
        residual_state,
        silu_low,
        modulation,
        normed_in,
        qkv_rows,
        log_total,
        attended,
        attn_out,
        middle,
        normed_mid,
        pre_act,
        activated,
        mlp_out,
    )
    return (result, stored)


def backward_layer(upstream, cond_part, gathered, stored):
    (
        adaln_weight,
        adaln_bias,
        qkv_weight,
        query_bias,
        value_bias,
        proj_weight,
        proj_bias,
        expand_weight,
        expand_bias,
        reduce_weight,
        reduce_bias,
    ) = gathered
    (
        residual_state,
        silu_low,
        modulation,
        normed_in,
        qkv_rows,
        log_total,
        attended,
        attn_out,
        middle,
        normed_mid,
        pre_act,
        activated,
        mlp_out,
    ) = stored
    latent_count, seq_len, model_width = residual_state.shape
    inv_root = HEAD ** (-0.5)
    shift_attn, scale_attn, gate_attn, shift_mlp, scale_mlp, gate_mlp = jnp.split(
        modulation, 6, axis=-1
    )
    d_mlp = (gate_mlp[:, None, :] * upstream).astype(jnp.bfloat16)
    d_gate_mlp = jnp.sum(upstream * mlp_out, axis=1)
    g_reduce_w = jnp.einsum("bsf,bsd->fd", activated, d_mlp, preferred_element_type=jnp.float32)
    g_reduce_b = jnp.sum(d_mlp, axis=(0, 1), dtype=jnp.float32)
    d_act = jnp.einsum("bsd,fd->bsf", d_mlp, reduce_weight, preferred_element_type=jnp.float32)
    _, pull_gelu = jax.vjp(gelu_tanh, pre_act)
    d_pre = pull_gelu(d_act)[0].astype(jnp.bfloat16)
    g_expand_w = jnp.einsum("bsd,bsf->df", normed_mid, d_pre, preferred_element_type=jnp.float32)
    g_expand_b = jnp.sum(d_pre, axis=(0, 1), dtype=jnp.float32)
    d_normed_mid = jnp.einsum(
        "bsf,df->bsd", d_pre, expand_weight, preferred_element_type=jnp.float32
    )
    _, pull_mid = jax.vjp(modulate, middle, shift_mlp, scale_mlp)
    d_middle, d_shift_mlp, d_scale_mlp = pull_mid(d_normed_mid)
    d_middle = d_middle + upstream
    d_attn = (gate_attn[:, None, :] * d_middle).astype(jnp.bfloat16)
    d_gate_attn = jnp.sum(d_middle * attn_out, axis=1)
    g_proj_w = jnp.einsum("bsd,bse->de", attended, d_attn, preferred_element_type=jnp.float32)
    g_proj_b = jnp.sum(d_attn, axis=(0, 1), dtype=jnp.float32)
    d_attended = jnp.einsum("bse,de->bsd", d_attn, proj_weight, preferred_element_type=jnp.float32)
    d_attended = d_attended.astype(jnp.bfloat16).reshape(latent_count, seq_len, HEADS, HEAD)
    queries = qkv_rows[:, :, 0]
    key_rows = qkv_rows[:, :, 1]
    value_rows = qkv_rows[:, :, 2]
    scores = (
        jnp.einsum("bqhe,bkhe->bhqk", queries, key_rows, preferred_element_type=jnp.float32)
        * inv_root
    )
    probs = jnp.exp(scores - log_total)
    d_probs = jnp.einsum(
        "bqhe,bkhe->bhqk", d_attended, value_rows, preferred_element_type=jnp.float32
    )
    d_scores = (probs * (d_probs - jnp.sum(probs * d_probs, axis=-1, keepdims=True))).astype(
        jnp.bfloat16
    )
    d_values = jnp.einsum(
        "bhqk,bqhe->bkhe",
        probs.astype(jnp.bfloat16),
        d_attended,
        preferred_element_type=jnp.float32,
    )
    d_queries = (
        jnp.einsum("bhqk,bkhe->bqhe", d_scores, key_rows, preferred_element_type=jnp.float32)
        * inv_root
    )
    d_keys = (
        jnp.einsum("bhqk,bqhe->bkhe", d_scores, queries, preferred_element_type=jnp.float32)
        * inv_root
    )
    d_qkv = jnp.stack([d_queries, d_keys, d_values], axis=2).astype(jnp.bfloat16)
    d_qkv = d_qkv.reshape(latent_count, seq_len, 3 * model_width)
    g_qkv_w = jnp.einsum("bsd,bsf->df", normed_in, d_qkv, preferred_element_type=jnp.float32)
    g_query_b = jnp.sum(d_qkv[:, :, :model_width], axis=(0, 1), dtype=jnp.float32)
    g_value_b = jnp.sum(d_qkv[:, :, 2 * model_width :], axis=(0, 1), dtype=jnp.float32)
    d_normed_in = jnp.einsum("bsf,df->bsd", d_qkv, qkv_weight, preferred_element_type=jnp.float32)
    _, pull_in = jax.vjp(modulate, residual_state, shift_attn, scale_attn)
    d_stream, d_shift_attn, d_scale_attn = pull_in(d_normed_in)
    d_stream = d_stream + d_middle
    d_modulation = jnp.concatenate(
        [d_shift_attn, d_scale_attn, d_gate_attn, d_shift_mlp, d_scale_mlp, d_gate_mlp], axis=-1
    ).astype(jnp.bfloat16)
    g_adaln_w = jnp.einsum("bd,bf->df", silu_low, d_modulation, preferred_element_type=jnp.float32)
    g_adaln_b = jnp.sum(d_modulation, axis=0, dtype=jnp.float32)
    d_silu = jnp.einsum("bf,df->bd", d_modulation, adaln_weight, preferred_element_type=jnp.float32)
    _, pull_silu = jax.vjp(jax.nn.silu, cond_part)
    d_cond = pull_silu(d_silu)[0]
    grads = (
        g_adaln_w,
        g_adaln_b,
        g_qkv_w,
        g_query_b,
        g_value_b,
        g_proj_w,
        g_proj_b,
        g_expand_w,
        g_expand_b,
        g_reduce_w,
        g_reduce_b,
    )
    return (d_stream, d_cond, grads)


def on_device(
    latents,
    conditioning,
    cotangent,
    adaln_weight,
    adaln_bias,
    qkv_weight,
    query_bias,
    value_bias,
    proj_weight,
    proj_bias,
    expand_weight,
    expand_bias,
    reduce_weight,
    reduce_bias,
):
    shards = (
        adaln_weight,
        adaln_bias,
        qkv_weight,
        query_bias,
        value_bias,
        proj_weight,
        proj_bias,
        expand_weight,
        expand_bias,
        reduce_weight,
        reduce_bias,
    )
    per_batch = latents.shape[0] // MB
    streams = [
        latents[batch_no * per_batch : (batch_no + 1) * per_batch].astype(jnp.float32)
        for batch_no in range(MB)
    ]
    cond_parts = [
        conditioning[batch_no * per_batch : (batch_no + 1) * per_batch].astype(jnp.float32)
        for batch_no in range(MB)
    ]
    stored = [[None] * LAYERS for batch_no in range(MB)]
    for batch_no in range(MB):
        for layer_number in range(LAYERS):
            gathered = fetch_forward(shards, layer_number)
            streams[batch_no], stored[batch_no][layer_number] = forward_layer(
                streams[batch_no], cond_parts[batch_no], gathered
            )
    outputs = jnp.concatenate(streams, axis=0).astype(jnp.bfloat16)
    upstream = [
        cotangent[batch_no * per_batch : (batch_no + 1) * per_batch].astype(jnp.float32)
        for batch_no in range(MB)
    ]
    cond_grads = [jnp.zeros_like(part) for part in cond_parts]
    totals = [None] * LAYERS
    summed = [None] * LAYERS

    def one_step(batch_no, layer_number, gathered):
        upstream[batch_no], cond_term, grads = backward_layer(
            upstream[batch_no], cond_parts[batch_no], gathered, stored[batch_no][layer_number]
        )
        cond_grads[batch_no] = cond_grads[batch_no] + cond_term
        if totals[layer_number] is None:
            totals[layer_number] = grads
        else:
            totals[layer_number] = tuple(
                (earlier + latest for earlier, latest in zip(totals[layer_number], grads))
            )

    for batch_no in range(MB):
        for layer_number in reversed(range(LAYERS)):
            gathered = fetch_backward(shards, layer_number)
            one_step(batch_no, layer_number, gathered)
    for layer_number in range(LAYERS):
        summed[layer_number] = send_grads(totals[layer_number])
    stacked = [
        jnp.stack([summed[layer_number][member] for layer_number in range(LAYERS)])
        for member in range(11)
    ]
    grad_latents = jnp.concatenate(upstream, axis=0)
    grad_conditioning = jnp.concatenate(cond_grads, axis=0)
    return tuple([outputs, grad_latents, grad_conditioning] + stacked)


def solution(mesh):
    in_specs = (
        P(("dp", "pair"), None, None),
        P(("dp", "pair"), None),
        P(("dp", "pair"), None, None),
        P(None, ("dp", "pair"), None),
        P(None, ("dp", "pair")),
        P(None, ("dp", "pair"), None),
        P(None, ("dp", "pair")),
        P(None, ("dp", "pair")),
        P(None, ("dp", "pair"), None),
        P(None, ("dp", "pair")),
        P(None, ("dp", "pair"), None),
        P(None, ("dp", "pair")),
        P(None, ("dp", "pair"), None),
        P(None, ("dp", "pair")),
    )
    out_specs = (
        P(("dp", "pair"), None, None),
        P(("dp", "pair"), None, None),
        P(("dp", "pair"), None),
        P(None, ("dp", "pair"), None),
        P(None, ("dp", "pair")),
        P(None, ("dp", "pair"), None),
        P(None, ("dp", "pair")),
        P(None, ("dp", "pair")),
        P(None, ("dp", "pair"), None),
        P(None, ("dp", "pair")),
        P(None, ("dp", "pair"), None),
        P(None, ("dp", "pair")),
        P(None, ("dp", "pair"), None),
        P(None, ("dp", "pair")),
    )
    return jax.shard_map(
        on_device, mesh=mesh, in_specs=in_specs, out_specs=out_specs, check_vma=False
    )
```

profile of v0, /device:TPU:0, one launch (start us, length us, event | category | flops | bytes accessed | tf_op | source)
XLA Modules:
  0.0 2355.9 jit_solution(14363333910226478229)
XLA Ops:
  22.9 44.2 %all-reduce.25 = (bf16[768]{0:T(1024)(128)(2,1)S(1)}, bf16[768]{0:T(1024)(128)(2,1)S(1)}, bf16[4608]{0:T(1024)(128)(2,1)S(1)}, bf16[4608]{0:T(1024)(128)(2,1)S(1...) all-reduce(bf16[768]{0:T(1024)(128)(2,1)S(1)} %dynamic-update-slice, ...), channel_id=6, replica_groups=mesh['dp'=16,'pair'=2] {'dp','pair'}, use_global_device_ids=true, to_apply=%add.2 | all-reduce | flops 21504 | bytes 86016 | tf_op jit(solution)/shard_map/all_gather | solution.py:48
  71.3 15.7 all-gather.33.cloned.1.call-done
  93.1 68.1 %all-gather.43.cloned.1.call-done = bf16[1,768,4608]{2,1,0:T(8,128)(2,1)} async-done(((bf16[1,24,4608]{2,1,0:T(8,128)(2,1)}), bf16[1,768,4608]{2,1,0:T(8,128)(2,1)}) %all-gather.43.cloned.1.call-update) | async-done | bytes 7077904 | tf_op jit(solution)/shard_map/all_gather | solution.py:44
  168.5 54.8 %all-gather.35.cloned.1.call-done = bf16[1,768,2304]{2,1,0:T(8,128)(2,1)} async-done(((bf16[1,24,2304]{2,1,0:T(8,128)(2,1)}), bf16[1,768,2304]{2,1,0:T(8,128)(2,1)}) %all-gather.35.cloned.1.call-update) | async-done | bytes 3538960 | tf_op jit(solution)/shard_map/all_gather | solution.py:46
  233.5 46.0 %all-gather.37.cloned.1.call-done = bf16[1,768,768]{2,1,0:T(8,128)(2,1)} async-done(((bf16[1,24,768]{2,1,0:T(8,128)(2,1)}), bf16[1,768,768]{2,1,0:T(8,128)(2,1)}) %all-gather.37.cloned.1.call-update) | async-done | bytes 1179664 | tf_op jit(solution)/shard_map/all_gather | solution.py:49
  284.5 60.8 %all-gather.39.cloned.1.call-done = bf16[1,768,3072]{2,1,0:T(8,128)(2,1)} async-done(((bf16[1,24,3072]{2,1,0:T(8,128)(2,1)}), bf16[1,768,3072]{2,1,0:T(8,128)(2,1)}) %all-gather.39.cloned.1.call-update) | async-done | bytes 4718608 | tf_op jit(solution)/shard_map/all_gather | solution.py:51
  351.1 59.5 %all-gather.41.cloned.1.call-done = bf16[1,3072,768]{2,1,0:T(8,128)(2,1)} async-done(((bf16[1,96,768]{2,1,0:T(8,128)(2,1)}), bf16[1,3072,768]{2,1,0:T(8,128)(2,1)}) %all-gather.41.cloned.1.call-update) | async-done | bytes 4718608 | tf_op jit(solution)/shard_map/all_gather | solution.py:53
  418.0 53.7 %all-gather.45.cloned.1.call-done = bf16[1,768,2304]{2,1,0:T(8,128)(2,1)} async-done(((bf16[1,24,2304]{2,1,0:T(8,128)(2,1)}), bf16[1,768,2304]{2,1,0:T(8,128)(2,1)}) %all-gather.45.cloned.1.call-update) | async-done | bytes 3538960 | tf_op jit(solution)/shard_map/all_gather | solution.py:46
  484.6 43.0 %all-gather.47.cloned.1.call-done = bf16[1,768,768]{2,1,0:T(8,128)(2,1)} async-done(((bf16[1,24,768]{2,1,0:T(8,128)(2,1)}), bf16[1,768,768]{2,1,0:T(8,128)(2,1)}) %all-gather.47.cloned.1.call-update) | async-done | bytes 1179664 | tf_op jit(solution)/shard_map/all_gather | solution.py:49
  532.2 60.7 %all-gather.49.cloned.1.call-done = bf16[1,768,3072]{2,1,0:T(8,128)(2,1)} async-done(((bf16[1,24,3072]{2,1,0:T(8,128)(2,1)}), bf16[1,768,3072]{2,1,0:T(8,128)(2,1)}) %all-gather.49.cloned.1.call-update) | async-done | bytes 4718608 | tf_op jit(solution)/shard_map/all_gather | solution.py:51
  598.6 59.5 %all-gather.51.cloned.1.call-done = bf16[1,3072,768]{2,1,0:T(8,128)(2,1)} async-done(((bf16[1,96,768]{2,1,0:T(8,128)(2,1)}), bf16[1,3072,768]{2,1,0:T(8,128)(2,1)}) %all-gather.51.cloned.1.call-update) | async-done | bytes 4718608 | tf_op jit(solution)/shard_map/all_gather | solution.py:53
  983.5 13.3 multiply_add_fusion.1
  996.8 14.2 reshape.2092
  1011.4 14.2 reshape.2093
  1055.1 39.7 %reduce-scatter.19.cloned.1.call-done = f32[144,128]{1,0:T(8,128)} async-done(((f32[4608,128]{1,0:T(8,128)}), f32[144,128]{1,0:T(8,128)}) %reduce-scatter.19.cloned.1.call-update) | async-done | bytes 73744 | tf_op jit(solution)/shard_map/reduce_scatter | solution.py:108
  1095.7 103.0 %reduce-scatter.21.cloned.1.call-done = f32[144,128]{1,0:T(8,128)} async-done(((f32[4608,128]{1,0:T(8,128)}), f32[144,128]{1,0:T(8,128)}) %reduce-scatter.21.cloned.1.call-update) | async-done | bytes 73744 | tf_op jit(solution)/shard_map/reduce_scatter | solution.py:108
  1200.3 122.5 %reduce-scatter.15.cloned.1.call-done = f32[432,128]{1,0:T(8,128)} async-done(((f32[13824,128]{1,0:T(8,128)}), f32[432,128]{1,0:T(8,128)}) %reduce-scatter.15.cloned.1.call-update) | async-done | bytes 221200 | tf_op jit(solution)/shard_map/reduce_scatter | solution.py:105
  1323.8 123.0 %reduce-scatter.17.cloned.1.call-done = f32[432,128]{1,0:T(8,128)} async-done(((f32[13824,128]{1,0:T(8,128)}), f32[432,128]{1,0:T(8,128)}) %reduce-scatter.17.cloned.1.call-update) | async-done | bytes 221200 | tf_op jit(solution)/shard_map/reduce_scatter | solution.py:105
  1448.7 139.1 %reduce-scatter.27.cloned.1.call-done = f32[576,128]{1,0:T(8,128)} async-done(((f32[18432,128]{1,0:T(8,128)}), f32[576,128]{1,0:T(8,128)}) %reduce-scatter.27.cloned.1.call-update) | async-done | bytes 294928 | tf_op jit(solution)/shard_map/reduce_scatter | solution.py:112
  1588.8 139.9 %reduce-scatter.29.cloned.1.call-done = f32[576,128]{1,0:T(8,128)} async-done(((f32[18432,128]{1,0:T(8,128)}), f32[576,128]{1,0:T(8,128)}) %reduce-scatter.29.cloned.1.call-update) | async-done | bytes 294928 | tf_op jit(solution)/shard_map/reduce_scatter | solution.py:112
  1729.7 139.9 %reduce-scatter.23.cloned.1.call-done = f32[576,128]{1,0:T(8,128)} async-done(((f32[18432,128]{1,0:T(8,128)}), f32[576,128]{1,0:T(8,128)}) %reduce-scatter.23.cloned.1.call-update) | async-done | bytes 294928 | tf_op jit(solution)/shard_map/reduce_scatter | solution.py:110
  1870.6 140.0 %reduce-scatter.25.cloned.1.call-done = f32[576,128]{1,0:T(8,128)} async-done(((f32[18432,128]{1,0:T(8,128)}), f32[576,128]{1,0:T(8,128)}) %reduce-scatter.25.cloned.1.call-update) | async-done | bytes 294928 | tf_op jit(solution)/shard_map/reduce_scatter | solution.py:110
  2013.4 165.1 %reduce-scatter.11.cloned.1.call-done = f32[864,128]{1,0:T(8,128)} async-done(((f32[27648,128]{1,0:T(8,128)}), f32[864,128]{1,0:T(8,128)}) %reduce-scatter.11.cloned.1.call-update) | async-done | bytes 442384 | tf_op jit(solution)/shard_map/reduce_scatter | solution.py:103
  2179.5 167.0 %reduce-scatter.13.cloned.1.call-done = f32[864,128]{1,0:T(8,128)} async-done(((f32[27648,128]{1,0:T(8,128)}), f32[864,128]{1,0:T(8,128)}) %reduce-scatter.13.cloned.1.call-update) | async-done | bytes 442384 | tf_op jit(solution)/shard_map/reduce_scatter | solution.py:103
  (962 shorter events, 450.2 us)
Async XLA Ops:
  7.3 79.8 %all-gather.33.cloned.1.call-start = ((), (), s32[]{:S(2)}) async-start(), calls=%async_computation.20 | async-start | bytes 7299072 | tf_op jit(solution)/shard_map/all_gather | solution.py:44
  9.2 151.9 %all-gather.43.cloned.1.call-start = ((), (), s32[]{:S(2)}) async-start(), calls=%async_computation.25 | async-start | bytes 7299072 | tf_op jit(solution)/shard_map/all_gather | solution.py:44
  10.0 213.3 %all-gather.35.cloned.1.call-start = ((), (), s32[]{:S(2)}) async-start(), calls=%async_computation.21 | async-start | bytes 3649536 | tf_op jit(solution)/shard_map/all_gather | solution.py:46
  11.7 267.8 %all-gather.37.cloned.1.call-start = ((), (), s32[]{:S(2)}) async-start(), calls=%async_computation.22 | async-start | bytes 1216512 | tf_op jit(solution)/shard_map/all_gather | solution.py:49
  13.2 332.1 %all-gather.39.cloned.1.call-start = ((), (), s32[]{:S(2)}) async-start(), calls=%async_computation.23 | async-start | bytes 4866048 | tf_op jit(solution)/shard_map/all_gather | solution.py:51
  15.0 395.6 %all-gather.41.cloned.1.call-start = ((), (), s32[]{:S(2)}) async-start(), calls=%async_computation.24 | async-start | bytes 4866048 | tf_op jit(solution)/shard_map/all_gather | solution.py:53
  16.8 455.0 %all-gather.45.cloned.1.call-start = ((), (), s32[]{:S(2)}) async-start(), calls=%async_computation.26 | async-start | bytes 3649536 | tf_op jit(solution)/shard_map/all_gather | solution.py:46
  17.5 510.0 %all-gather.47.cloned.1.call-start = ((), (), s32[]{:S(2)}) async-start(), calls=%async_computation.27 | async-start | bytes 1216512 | tf_op jit(solution)/shard_map/all_gather | solution.py:49
  18.3 574.7 %all-gather.49.cloned.1.call-start = ((), (), s32[]{:S(2)}) async-start(), calls=%async_computation.28 | async-start | bytes 4866048 | tf_op jit(solution)/shard_map/all_gather | solution.py:51
  19.0 639.1 %all-gather.51.cloned.1.call-start = ((), (), s32[]{:S(2)}) async-start(), calls=%async_computation.29 | async-start | bytes 4866048 | tf_op jit(solution)/shard_map/all_gather | solution.py:53
  19.6 1023.0 %all-reduce.28.cloned.1.call-start = ((), (), s32[]{:S(2)}) async-start(), calls=%async_computation.30 | async-start | bytes 196608
  20.0 203.3 %copy-start.166 = (f32[256]{0:T(256)}, f32[256]{0:T(256)S(1)}, u32[]{:S(2)}) copy-start(f32[256]{0:T(256)S(1)} %broadcast_multiply_fusion.7) | copy-start | bytes 3076
  228.8 243.0 %copy-start.123 = (f32[768]{0:T(1024)}, f32[768]{0:T(1024)S(1)}, u32[]{:S(2)}) copy-start(f32[768]{0:T(1024)S(1)} %get-tuple-element.51) | copy-start | bytes 9220
  228.8 243.0 %copy-start.140 = (f32[768]{0:T(1024)}, f32[768]{0:T(1024)S(1)}, u32[]{:S(2)}) copy-start(f32[768]{0:T(1024)S(1)} %get-tuple-element.50) | copy-start | bytes 9220
  860.5 234.3 %reduce-scatter.19.cloned.1.call-start = ((), (), s32[]{:S(2)}) async-start(), calls=%async_computation.14 | async-start | bytes 2433024 | tf_op jit(solution)/shard_map/reduce_scatter | solution.py:108
  866.8 331.9 %reduce-scatter.21.cloned.1.call-start = ((), (), s32[]{:S(2)}) async-start(), calls=%async_computation.15 | async-start | bytes 2433024 | tf_op jit(solution)/shard_map/reduce_scatter | solution.py:108
  870.9 452.0 %reduce-scatter.15.cloned.1.call-start = ((), (), s32[]{:S(2)}) async-start(), calls=%async_computation.12 | async-start | bytes 7299072 | tf_op jit(solution)/shard_map/reduce_scatter | solution.py:105
  885.6 561.2 %reduce-scatter.17.cloned.1.call-start = ((), (), s32[]{:S(2)}) async-start(), calls=%async_computation.13 | async-start | bytes 7299072 | tf_op jit(solution)/shard_map/reduce_scatter | solution.py:105
  900.6 687.2 %reduce-scatter.27.cloned.1.call-start = ((), (), s32[]{:S(2)}) async-start(), calls=%async_computation.18 | async-start | bytes 9732096 | tf_op jit(solution)/shard_map/reduce_scatter | solution.py:112
  921.5 807.1 %reduce-scatter.29.cloned.1.call-start = ((), (), s32[]{:S(2)}) async-start(), calls=%async_computation.19 | async-start | bytes 9732096 | tf_op jit(solution)/shard_map/reduce_scatter | solution.py:112
  943.7 925.9 %reduce-scatter.23.cloned.1.call-start = ((), (), s32[]{:S(2)}) async-start(), calls=%async_computation.16 | async-start | bytes 9732096 | tf_op jit(solution)/shard_map/reduce_scatter | solution.py:110
  963.2 1047.4 %reduce-scatter.25.cloned.1.call-start = ((), (), s32[]{:S(2)}) async-start(), calls=%async_computation.17 | async-start | bytes 9732096 | tf_op jit(solution)/shard_map/reduce_scatter | solution.py:110
  982.7 1195.7 %reduce-scatter.11.cloned.1.call-start = ((), (), s32[]{:S(2)}) async-start(), calls=%async_computation.10 | async-start | bytes 14598144 | tf_op jit(solution)/shard_map/reduce_scatter | solution.py:103
  1011.0 1335.5 %reduce-scatter.13.cloned.1.call-start = ((), (), s32[]{:S(2)}) async-start(), calls=%async_computation.11 | async-start | bytes 14598144 | tf_op jit(solution)/shard_map/reduce_scatter | solution.py:103
  (293 other events, 2442.0 us)
Sparse Core Ops, SparseCore 0:
  11.6 75.4 all-gather.32
  90.5 70.5 all-gather.42
  164.7 58.5 all-gather.34
  226.6 52.8 all-gather.36
  282.8 62.4 all-gather.38
  348.7 61.8 all-gather.40
  413.5 58.2 all-gather.44
  474.7 52.8 all-gather.46
  530.5 62.4 all-gather.48
  596.3 61.8 all-gather.50
  860.7 128.1 all-reduce.27
  994.0 100.7 reduce-scatter.18
  1100.1 98.6 reduce-scatter.20
  1204.3 118.5 reduce-scatter.14
  1328.4 118.4 reduce-scatter.16
  1452.6 135.1 reduce-scatter.26
  1593.5 135.1 reduce-scatter.28
  1734.4 135.1 reduce-scatter.22
  1875.5 135.1 reduce-scatter.24
  2016.5 161.8 reduce-scatter.10
  2184.4 162.0 reduce-scatter.12
where the time goes:
time: 2370 us; the launch traced here: 2360 us
  waiting for transfers between devices  1800 us (76%)
  local copies, waits for them, and re-layouts  203 us (9%)
  matrix products  196 us (8%)
  other arithmetic  87.8 us (4%)
  blocking collectives  44.2 us (2%)
    reduce_scatter x2, waiting for transfers between devices, send_grads(): lax.psum_scatter(flat[0], ('dp', 'pair'), scatter_dimension=0, tiled=True)  332 us
    reduce_scatter x2, waiting for transfers between devices, send_grads(): lax.psum_scatter(flat[7], ('dp', 'pair'), scatter_dimension=0, tiled=True)  280 us
    reduce_scatter x2, waiting for transfers between devices, send_grads(): lax.psum_scatter(flat[9], ('dp', 'pair'), scatter_dimension=0, tiled=True)  279 us
    reduce_scatter x2, waiting for transfers between devices, send_grads(): lax.psum_scatter(flat[2], ('dp', 'pair'), scatter_dimension=0, tiled=True)  246 us
    reduce_scatter x2, waiting for transfers between devices, send_grads(): lax.psum_scatter(flat[5], ('dp', 'pair'), scatter_dimension=0, tiled=True)  143 us
    all_gather x2, waiting for transfers between devices, fetch_forward(): lax.all_gather(expand_weight[layer_number], ('dp', 'pair'), axis=0, tiled...  122 us
    all_gather x2, waiting for transfers between devices, fetch_forward(): lax.all_gather(reduce_weight[layer_number], ('dp', 'pair'), axis=0, tiled...  119 us
    all_gather x2, waiting for transfers between devices, fetch_forward(): lax.all_gather(qkv_weight[layer_number], ('dp', 'pair'), axis=0, tiled=True)  109 us
  transfers between devices with their start and end apart: 21, of which 20 were waited for; matrix products, arithmetic and copies ran while one was open for 11% of the time, Pallas kernels for 0%

commit v1 on v0

--- a/solution.py
+++ b/solution.py
@@ -6,7 +6,6 @@
 HEADS = 12
 HEAD = 64
 LAYERS = 2
-MB = 2
 
 
 EPSILON = 1e-06
@@ -26,7 +25,12 @@
     return jax.nn.gelu(values, approximate=True)
 
 
-def fetch_forward(shards, layer_number):
+AXES = ("dp", "pair")
+LANES = 128
+GRAD_DTYPE = jnp.bfloat16
+
+
+def pack_shards(shards, layer_number):
     (
         adaln_weight,
         adaln_bias,
@@ -39,23 +43,58 @@
         expand_bias,
         reduce_weight,
         reduce_bias,
-    ) = shards
+    ) = [member[layer_number] for member in shards]
+    rows = qkv_weight.shape[0]
+    pieces = reduce_weight.shape[0] // rows
+    biases = jnp.concatenate(
+        [adaln_bias, query_bias, value_bias, proj_bias, expand_bias, reduce_bias]
+    )
+    biases = jnp.pad(biases, (0, rows * LANES - biases.shape[0])).reshape(rows, LANES)
+    reduce_parts = [reduce_weight[piece * rows : (piece + 1) * rows] for piece in range(pieces)]
+    return jnp.concatenate(
+        [adaln_weight, qkv_weight, proj_weight, expand_weight] + reduce_parts + [biases], axis=1
+    )
+
+
+def fetch(shards, layer_number, shard_count):
+    block = pack_shards(shards, layer_number)
+    rows = block.shape[0]
+    full = lax.all_gather(block, AXES, axis=0, tiled=True)
+    widths = [shards[0].shape[2], shards[2].shape[2], shards[5].shape[2], shards[7].shape[2]]
+    weights = []
+    at = 0
+    for width in widths:
+        weights.append(full[:, at : at + width])
+        at += width
+    reduce_cols = shards[9].shape[2]
+    pieces = shards[9].shape[1] // rows
+    reduce_weight = full[:, at : at + pieces * reduce_cols]
+    reduce_weight = reduce_weight.reshape(shard_count, rows, pieces, reduce_cols)
+    reduce_weight = reduce_weight.transpose(0, 2, 1, 3).reshape(-1, reduce_cols)
+    at += pieces * reduce_cols
+    flat = full[:, at:].reshape(shard_count, rows * LANES)
+    biases = []
+    at = 0
+    for member in (1, 3, 4, 6, 8, 10):
+        size = shards[member].shape[1]
+        biases.append(flat[:, at : at + size].reshape(-1))
+        at += size
     return (
-        lax.all_gather(adaln_weight[layer_number], ("dp", "pair"), axis=0, tiled=True),
-        lax.all_gather(adaln_bias[layer_number], ("dp", "pair"), axis=0, tiled=True),
-        lax.all_gather(qkv_weight[layer_number], ("dp", "pair"), axis=0, tiled=True),
-        lax.all_gather(query_bias[layer_number], ("dp", "pair"), axis=0, tiled=True),
-        lax.all_gather(value_bias[layer_number], ("dp", "pair"), axis=0, tiled=True),
-        lax.all_gather(proj_weight[layer_number], ("dp", "pair"), axis=0, tiled=True),
-        lax.all_gather(proj_bias[layer_number], ("dp", "pair"), axis=0, tiled=True),
-        lax.all_gather(expand_weight[layer_number], ("dp", "pair"), axis=0, tiled=True),
-        lax.all_gather(expand_bias[layer_number], ("dp", "pair"), axis=0, tiled=True),
-        lax.all_gather(reduce_weight[layer_number], ("dp", "pair"), axis=0, tiled=True),
-        lax.all_gather(reduce_bias[layer_number], ("dp", "pair"), axis=0, tiled=True),
-    )
-
-
-def fetch_backward(shards, layer_number):
+        weights[0],
+        biases[0],
+        weights[1],
+        biases[1],
+        biases[2],
+        weights[2],
+        biases[3],
+        weights[3],
+        biases[4],
+        reduce_weight,
+        biases[5],
+    )
+
+
+def send_grads(totals, shard_count):
     (
         adaln_weight,
         adaln_bias,
@@ -68,51 +107,55 @@
         expand_bias,
         reduce_weight,
         reduce_bias,
-    ) = shards
+    ) = totals
+    model_width = qkv_weight.shape[0]
+    rows = model_width // shard_count
+    reduce_cols = reduce_weight.shape[1]
+    pieces = reduce_weight.shape[0] // model_width
+    biases = [adaln_bias, query_bias, value_bias, proj_bias, expand_bias, reduce_bias]
+    flat = jnp.concatenate([member.reshape(shard_count, -1) for member in biases], axis=1)
+    bias_sizes = [member.shape[0] // shard_count for member in biases]
+    flat = jnp.pad(flat, ((0, 0), (0, rows * LANES - flat.shape[1])))
+    flat = flat.astype(GRAD_DTYPE).reshape(model_width, LANES)
+    split = reduce_weight.astype(GRAD_DTYPE).reshape(shard_count, pieces, rows, reduce_cols)
+    split = split.transpose(0, 2, 1, 3).reshape(model_width, pieces * reduce_cols)
+    weights = [adaln_weight, qkv_weight, proj_weight, expand_weight]
+    block = jnp.concatenate(
+        [member.astype(GRAD_DTYPE) for member in weights] + [split, flat], axis=1
+    )
+    mine = lax.psum_scatter(block, AXES, scatter_dimension=0, tiled=True).astype(jnp.float32)
+    out = []
+    at = 0
+    for member in weights:
+        out.append(mine[:, at : at + member.shape[1]])
+        at += member.shape[1]
+    reduced = jnp.concatenate(
+        [
+            mine[:, at + piece * reduce_cols : at + (piece + 1) * reduce_cols]
+            for piece in range(pieces)
+        ],
+        axis=0,
+    )
+    at += pieces * reduce_cols
+    flat = mine[:, at:].reshape(-1)
+    small = []
+    at = 0
+    for size in bias_sizes:
+        small.append(flat[at : at + size])
+        at += size
     return (
-        lax.all_gather(adaln_weight[layer_number], ("dp", "pair"), axis=0, tiled=True),
-        lax.all_gather(adaln_bias[layer_number], ("dp", "pair"), axis=0, tiled=True),
-        lax.all_gather(qkv_weight[layer_number], ("dp", "pair"), axis=0, tiled=True),
-        lax.all_gather(query_bias[layer_number], ("dp", "pair"), axis=0, tiled=True),
-        lax.all_gather(value_bias[layer_number], ("dp", "pair"), axis=0, tiled=True),
-        lax.all_gather(proj_weight[layer_number], ("dp", "pair"), axis=0, tiled=True),
-        lax.all_gather(proj_bias[layer_number], ("dp", "pair"), axis=0, tiled=True),
-        lax.all_gather(expand_weight[layer_number], ("dp", "pair"), axis=0, tiled=True),
-        lax.all_gather(expand_bias[layer_number], ("dp", "pair"), axis=0, tiled=True),
-        lax.all_gather(reduce_weight[layer_number], ("dp", "pair"), axis=0, tiled=True),
-        lax.all_gather(reduce_bias[layer_number], ("dp", "pair"), axis=0, tiled=True),
-    )
-
-
-def tile_rows(matrix):
-    if matrix.ndim == 2:
-        return matrix.reshape(matrix.shape[0] * matrix.shape[1] // 128, 128)
-    return matrix
-
-
-def untile_rows(matrix, columns):
-    if columns > 0:
-        return matrix.reshape(-1, columns)
-    return matrix
-
-
-def send_grads(totals):
-    widths = [member.shape[1] if member.ndim == 2 else 0 for member in totals]
-    flat = [tile_rows(member) for member in totals]
-    summed = (
-        lax.psum_scatter(flat[0], ("dp", "pair"), scatter_dimension=0, tiled=True),
-        lax.psum_scatter(flat[1], ("dp", "pair"), scatter_dimension=0, tiled=True),
-        lax.psum_scatter(flat[2], ("dp", "pair"), scatter_dimension=0, tiled=True),
-        lax.psum_scatter(flat[3], ("dp", "pair"), scatter_dimension=0, tiled=True),
-        lax.psum_scatter(flat[4], ("dp", "pair"), scatter_dimension=0, tiled=True),
-        lax.psum_scatter(flat[5], ("dp", "pair"), scatter_dimension=0, tiled=True),
-        lax.psum_scatter(flat[6], ("dp", "pair"), scatter_dimension=0, tiled=True),
-        lax.psum_scatter(flat[7], ("dp", "pair"), scatter_dimension=0, tiled=True),
-        lax.psum_scatter(flat[8], ("dp", "pair"), scatter_dimension=0, tiled=True),
-        lax.psum_scatter(flat[9], ("dp", "pair"), scatter_dimension=0, tiled=True),
-        lax.psum_scatter(flat[10], ("dp", "pair"), scatter_dimension=0, tiled=True),
-    )
-    return tuple((untile_rows(member, columns) for member, columns in zip(summed, widths)))
+        out[0],
+        small[0],
+        out[1],
+        small[1],
+        small[2],
+        out[2],
+        small[3],
+        out[3],
+        small[4],
+        reduced,
+        small[5],
+    )
 
 
 def forward_layer(residual_state, cond_part, gathered):
@@ -343,56 +386,28 @@
         reduce_weight,
         reduce_bias,
     )
-    per_batch = latents.shape[0] // MB
-    streams = [
-        latents[batch_no * per_batch : (batch_no + 1) * per_batch].astype(jnp.float32)
-        for batch_no in range(MB)
-    ]
-    cond_parts = [
-        conditioning[batch_no * per_batch : (batch_no + 1) * per_batch].astype(jnp.float32)
-        for batch_no in range(MB)
-    ]
-    stored = [[None] * LAYERS for batch_no in range(MB)]
-    for batch_no in range(MB):
-        for layer_number in range(LAYERS):
-            gathered = fetch_forward(shards, layer_number)
-            streams[batch_no], stored[batch_no][layer_number] = forward_layer(
-                streams[batch_no], cond_parts[batch_no], gathered
-            )
-    outputs = jnp.concatenate(streams, axis=0).astype(jnp.bfloat16)
-    upstream = [
-        cotangent[batch_no * per_batch : (batch_no + 1) * per_batch].astype(jnp.float32)
-        for batch_no in range(MB)
-    ]
-    cond_grads = [jnp.zeros_like(part) for part in cond_parts]
-    totals = [None] * LAYERS
+    shard_count = lax.axis_size(AXES)
+    stream = latents.astype(jnp.float32)
+    cond_part = conditioning.astype(jnp.float32)
+    gathered = [fetch(shards, layer_number, shard_count) for layer_number in range(LAYERS)]
+    stored = [None] * LAYERS
+    for layer_number in range(LAYERS):
+        stream, stored[layer_number] = forward_layer(stream, cond_part, gathered[layer_number])
+    outputs = stream.astype(jnp.bfloat16)
+    upstream = cotangent.astype(jnp.float32)
+    grad_conditioning = jnp.zeros_like(cond_part)
     summed = [None] * LAYERS
-
-    def one_step(batch_no, layer_number, gathered):
-        upstream[batch_no], cond_term, grads = backward_layer(
-            upstream[batch_no], cond_parts[batch_no], gathered, stored[batch_no][layer_number]
+    for layer_number in reversed(range(LAYERS)):
+        upstream, cond_term, grads = backward_layer(
+            upstream, cond_part, gathered[layer_number], stored[layer_number]
         )
-        cond_grads[batch_no] = cond_grads[batch_no] + cond_term
-        if totals[layer_number] is None:
-            totals[layer_number] = grads
-        else:
-            totals[layer_number] = tuple(
-                (earlier + latest for earlier, latest in zip(totals[layer_number], grads))
-            )
-
-    for batch_no in range(MB):
-        for layer_number in reversed(range(LAYERS)):
-            gathered = fetch_backward(shards, layer_number)
-            one_step(batch_no, layer_number, gathered)
-    for layer_number in range(LAYERS):
-        summed[layer_number] = send_grads(totals[layer_number])
+        grad_conditioning = grad_conditioning + cond_term
+        summed[layer_number] = send_grads(grads, shard_count)
     stacked = [
         jnp.stack([summed[layer_number][member] for layer_number in range(LAYERS)])
         for member in range(11)
     ]
-    grad_latents = jnp.concatenate(upstream, axis=0)
-    grad_conditioning = jnp.concatenate(cond_grads, axis=0)
-    return tuple([outputs, grad_latents, grad_conditioning] + stacked)
+    return tuple([outputs, upstream, grad_conditioning] + stacked)
 
 
 def solution(mesh):

time: 2370 us -> 988 us (0.42)
  waiting for transfers between devices: 1800 us -> 651 us
  local copies, waits for them, and re-layouts: 203 us -> 96 us
  other arithmetic: 87.8 us -> 31.4 us
  blocking collectives: 44.2 us -> 0 us
    reduce_scatter x10 -> x0, waiting for transfers between devices: 1280 us -> none  [the longest x2 332 us: send_grads(): lax.psum_scatter(flat[0], ('dp', 'pair'), scatter_dimension=0, tiled=True)]
    unnamed x22 -> x6, waiting for transfers between devices: 3.57 us -> 379 us
    all_gather x10 -> x2, waiting for transfers between devices: 522 us -> 273 us  [fetch(): full = lax.all_gather(block, AXES, axis=0, tiled=True)]
    reshape x10 -> x22, local copies, waits for them, and re-layouts: 92.3 us -> 28 us  [the longest x2 19.5 us: fetch(): reduce_weight.reshape(shard_count, rows, pieces, reduce_cols)]
    all_gather x1 -> x0, blocking collectives: 44.2 us -> none  [fetch_forward(): lax.all_gather(value_bias[layer_number], ('dp', 'pair'), axis=0, tiled=True)]
    unnamed x644 -> x234, local copies, waits for them, and re-layouts: 64.2 us -> 29.3 us
    add x14 -> x0, other arithmetic: 28.7 us -> none  [the longest x13 28.1 us: one_step(): earlier + latest]
  transfers between devices with their start and end apart: 21 -> 4, of which waited for: 20 -> 4; matrix products, arithmetic and copies ran while one was open for 11% -> 6% of each run, Pallas kernels for 0% -> 0%
where the time goes in v1:
time: 988 us; the launch traced here: 982 us
  waiting for transfers between devices  651 us (66%)
  matrix products  188 us (19%)
  local copies, waits for them, and re-layouts  96 us (10%)
  other arithmetic  31.4 us (3%)
  between operations  15.8 us (2%)
    unnamed x6, waiting for transfers between devices  379 us
    all_gather x2, waiting for transfers between devices, fetch(): full = lax.all_gather(block, AXES, axis=0, tiled=True)  273 us
    unnamed x234, local copies, waits for them, and re-layouts  29.3 us
  transfers between devices with their start and end apart: 4, of which 4 were waited for; matrix products, arithmetic and copies ran while one was open for 6% of the time, Pallas kernels for 0%

profile of v1, /device:TPU:0, one launch (start us, length us, event | category | flops | bytes accessed | tf_op | source)
XLA Modules:
  0.0 982.5 jit_solution(2211317118282993080)
XLA Ops:
  20.5 136.7 %all-gather.5.cloned.1.call-done = bf16[768,13952]{1,0:T(8,128)(2,1)} async-done(((bf16[24,13952]{1,0:T(8,128)(2,1)}), bf16[768,13952]{1,0:T(8,128)(2,1)}) %all-gather.5.cloned.1.call-update) | async-done | bytes 21430288 | tf_op jit(solution)/shard_map/all_gather | solution.py:62
  159.0 136.0 %all-gather.3.cloned.1.call-done = bf16[768,13952]{1,0:T(8,128)(2,1)} async-done(((bf16[24,13952]{1,0:T(8,128)(2,1)}), bf16[768,13952]{1,0:T(8,128)(2,1)}) %all-gather.3.cloned.1.call-update) | async-done | bytes 21430288 | tf_op jit(solution)/shard_map/all_gather | solution.py:62
  300.7 5.5 fusion.36
  324.6 9.8 reshape.428
  342.3 5.4 fusion.41
  347.7 5.2 fusion.135
  353.3 5.7 fusion.37
  375.9 9.7 reshape.434
  398.5 7.3 fusion.141
  405.9 7.1 multiply_reduce_fusion.7
  421.1 5.3 fusion.83
  437.1 5.4 multiply_reduce_fusion.11
  445.7 6.6 fusion.142
  452.4 5.6 bitcast_convert_fusion.2
  458.0 5.1 multiply_reduce_fusion.10
  472.3 5.3 fusion.86
  495.7 5.1 fusion.1
  509.6 5.1 fusion.34
  525.9 7.0 bitcast_convert_fusion
  541.0 11.8 %fusion.68 = (bf16[2,768]{1,0:T(2,128)(2,1)S(1)}, bf16[2,768]{1,0:T(2,128)(2,1)S(1)}, bf16[2,256,768]{2,1,0:T(8,128)(2,1)}) fusion(bf16[2,256,768]{2,1,0:T(8,128)(2,1)S(1)} %copy-done.28, f32[768]{0:T(1024)S(1)} %reshape.465, f32[2,256,768]{2,1,0:T(8,128)} %get-tuple-element.124, f32[2,256,768]{2,1,0:T(8,128)} %copy-done.14, f32[2,256]{1,0:T(2,128)S(1)} %copy-done.66, ...), kind=kOutput, calls=%fused_computation.108 | convolution fusion | flops 2435970048 | bytes 17331200 | tf_op jit(solution)/shard_map/dot_general | solution.py:222
  553.3 5.4 fusion
  578.0 6.5 fusion.111
  584.5 156.2 %reduce-scatter.7.cloned.1.call-done = bf16[24,13952]{1,0:T(8,128)(2,1)} async-done(((bf16[768,13952]{1,0:T(8,128)(2,1)}), bf16[24,13952]{1,0:T(8,128)(2,1)}) %reduce-scatter.7.cloned.1.call-update) | async-done | bytes 669712
  742.2 222.5 %reduce-scatter.9.cloned.1.call-done = bf16[24,13952]{1,0:T(8,128)(2,1)} async-done(((bf16[768,13952]{1,0:T(8,128)(2,1)}), bf16[24,13952]{1,0:T(8,128)(2,1)}) %reduce-scatter.9.cloned.1.call-update) | async-done | bytes 669712
  (415 shorter events, 185.3 us)
Async XLA Ops:
  7.2 150.0 %all-gather.5.cloned.1.call-start = ((), (), s32[]{:S(2)}) async-start(), calls=%async_computation.3 | async-start | bytes 22099968 | tf_op jit(solution)/shard_map/all_gather | solution.py:62
  12.3 284.3 %copy-start.67 = (bf16[2,768]{1,0:T(2,128)(2,1)S(1)}, bf16[2,768]{1,0:T(2,128)(2,1)}, u32[]{:S(2)}) copy-start(bf16[2,768]{1,0:T(2,128)(2,1)} %param.15) | copy-start | bytes 9220
  18.2 276.7 %all-gather.3.cloned.1.call-start = ((), (), s32[]{:S(2)}) async-start(), calls=%async_computation.2 | async-start | bytes 22099968 | tf_op jit(solution)/shard_map/all_gather | solution.py:62
  19.3 721.4 %reduce-scatter.7.cloned.1.call-start = ((), (), s32[]{:S(2)}) async-start(), calls=%async_computation.4 | async-start | bytes 22099968
  19.5 281.2 %copy-start.45 = (f32[2,256]{1,0:T(2,128)}, f32[2,256]{1,0:T(2,128)S(1)}, u32[]{:S(2)}) copy-start(f32[2,256]{1,0:T(2,128)S(1)} %broadcast_multiply_fusion.3) | copy-start | bytes 6148
  20.5 280.2 %copy-start.61 = (f32[2,256]{1,0:T(2,128)}, f32[2,256]{1,0:T(2,128)S(1)}, u32[]{:S(2)}) copy-start(f32[2,256]{1,0:T(2,128)S(1)} %fusion.116) | copy-start | bytes 6148
  300.7 41.6 %copy-start.82 = (f32[2,768]{1,0:T(2,128)}, f32[2,768]{1,0:T(2,128)S(1)}, u32[]{:S(2)}) copy-start(f32[2,768]{1,0:T(2,128)S(1)} %get-tuple-element.93) | copy-start | bytes 18436
  319.5 33.8 %copy-start.80 = (f32[2,768]{1,0:T(2,128)}, f32[2,768]{1,0:T(2,128)S(1)}, u32[]{:S(2)}) copy-start(f32[2,768]{1,0:T(2,128)S(1)} %get-tuple-element.89) | copy-start | bytes 18436
  319.5 74.0 %copy-start.78 = (f32[2,768]{1,0:T(2,128)}, f32[2,768]{1,0:T(2,128)S(1)}, u32[]{:S(2)}) copy-start(f32[2,768]{1,0:T(2,128)S(1)} %get-tuple-element.87) | copy-start | bytes 18436
  319.5 93.5 %copy-start.51 = (f32[2,768]{1,0:T(2,128)}, f32[2,768]{1,0:T(2,128)S(1)}, u32[]{:S(2)}) copy-start(f32[2,768]{1,0:T(2,128)S(1)} %get-tuple-element.88) | copy-start | bytes 18436
  319.5 124.4 %copy-start.53 = (f32[2,768]{1,0:T(2,128)}, f32[2,768]{1,0:T(2,128)S(1)}, u32[]{:S(2)}) copy-start(f32[2,768]{1,0:T(2,128)S(1)} %get-tuple-element.86) | copy-start | bytes 18436
  341.9 122.1 %copy-start.43 = (f32[2,256]{1,0:T(2,128)}, f32[2,256]{1,0:T(2,128)S(1)}, u32[]{:S(2)}) copy-start(f32[2,256]{1,0:T(2,128)S(1)} %broadcast_multiply_fusion.2) | copy-start | bytes 6148
  342.2 121.8 %copy-start.57 = (f32[2,256]{1,0:T(2,128)}, f32[2,256]{1,0:T(2,128)S(1)}, u32[]{:S(2)}) copy-start(f32[2,256]{1,0:T(2,128)S(1)} %fusion.117) | copy-start | bytes 6148
  352.9 36.0 %copy-start.5 = (f32[2,256,768]{2,1,0:T(8,128)}, f32[2,256,768]{2,1,0:T(8,128)S(1)}, u32[]{:S(2)}) copy-start(f32[2,256,768]{2,1,0:T(8,128)S(1)} %get-tuple-element.47) | copy-start | bytes 4718596
  352.9 90.9 %copy-start.47 = (f32[2,256]{1,0:T(2,128)}, f32[2,256]{1,0:T(2,128)S(1)}, u32[]{:S(2)}) copy-start(f32[2,256]{1,0:T(2,128)S(1)} %broadcast_multiply_fusion.1) | copy-start | bytes 6148
  353.3 90.6 %copy-start.63 = (f32[2,256]{1,0:T(2,128)}, f32[2,256]{1,0:T(2,128)S(1)}, u32[]{:S(2)}) copy-start(f32[2,256]{1,0:T(2,128)S(1)} %fusion.118) | copy-start | bytes 6148
  370.9 18.1 %copy-start.38 = (bf16[2,12,64,256]{3,2,1,0:T(8,128)(2,1)}, bf16[2,12,64,256]{3,2,1,0:T(8,128)(2,1)S(1)}, u32[]{:S(2)}) copy-start(bf16[2,12,64,256]{3,2,1,0:T(8,128)(2,1)S(1)} %fusion.71) | copy-start | bytes 2359300
  370.9 27.6 %copy-start.72 = (f32[3072]{0:T(1024)}, f32[3072]{0:T(1024)S(1)}, u32[]{:S(2)}) copy-start(f32[3072]{0:T(1024)S(1)} %reshape.464) | copy-start | bytes 36868
  393.2 19.8 %copy-start.10 = (f32[2,256,768]{2,1,0:T(8,128)}, f32[2,256,768]{2,1,0:T(8,128)S(1)}, u32[]{:S(2)}) copy-start(f32[2,256,768]{2,1,0:T(8,128)S(1)} %get-tuple-element.45) | copy-start | bytes 4718596
  393.2 19.8 %copy-start.55 = (f32[2,256]{1,0:T(2,128)}, f32[2,256]{1,0:T(2,128)S(1)}, u32[]{:S(2)}) copy-start(f32[2,256]{1,0:T(2,128)S(1)} %broadcast_multiply_fusion) | copy-start | bytes 6148
  393.5 19.5 %copy-start.74 = (f32[2,256]{1,0:T(2,128)}, f32[2,256]{1,0:T(2,128)S(1)}, u32[]{:S(2)}) copy-start(f32[2,256]{1,0:T(2,128)S(1)} %fusion.119) | copy-start | bytes 6148
  413.6 30.2 %copy-start.65 = (f32[2,256]{1,0:T(2,128)}, f32[2,256]{1,0:T(2,128)S(1)}, u32[]{:S(2)}) copy-start(f32[2,256]{1,0:T(2,128)S(1)} %negate_multiply_fusion.3) | copy-start | bytes 6148
  445.7 18.4 %copy-start.12 = (f32[2,256,768]{2,1,0:T(8,128)}, f32[2,256,768]{2,1,0:T(8,128)S(1)}, u32[]{:S(2)}) copy-start(f32[2,256,768]{2,1,0:T(8,128)S(1)} %get-tuple-element.36) | copy-start | bytes 4718596
  524.7 439.9 %reduce-scatter.9.cloned.1.call-start = ((), (), s32[]{:S(2)}) async-start(), calls=%async_computation.5 | async-start | bytes 22099968
  (86 other events, 419.2 us)
Sparse Core Ops, SparseCore 0:
  18.4 138.7 all-gather.4
  160.7 134.2 all-gather.2
  524.9 215.8 reduce-scatter.6
  747.0 217.6 reduce-scatter.8
